TPU v7x, 32 devices: a whole 2x2x4 slice. The times are simulated.
32 devices in a mesh: outer: 4 (over y, x), inner: 8 (over z, core).
Axes of the slice: x: 2, y: 2, z: 4, core: 2. Of those that a mesh axis runs over, the one named last changes fastest.
Arguments:
- query_rows: bfloat16 [8192, 64], P(('outer', 'inner')), may hold values from -40 to 40, as said below
- key_rows: bfloat16 [8192, 64], P(('outer', 'inner')), may hold values from -40 to 40, as said below
- value_rows: bfloat16 [8192, 512], P(('outer', 'inner')), may hold values from -9 to 9, as said below
Outputs:
- linear_out: bfloat16 [8192, 512], P(('outer', 'inner'))
- window_out: bfloat16 [8192, 512], P(('outer', 'inner'))
Inputs may be any that keep to these rules, and one draw needn't show every extreme that they name: `query_rows`: real-valued queries of each head. `key_rows`: real-valued keys of each head. `value_rows`: real-valued values.
All inputs are finite; a program needn't handle non-finite values.
Results may differ from a plain program's by a relative error of at most 0.0015.
The roundings to bfloat16 on the way count: a program that leaves them out, or rounds other values in their place, can miss the bound.
Values may be sent and summed in bfloat16 or wider, within the bound.
A program may use at most 128 MiB of HBM per device.

v0:
```python
import math

import jax
import jax.numpy as jnp
from jax import lax
from jax.sharding import PartitionSpec as P

H = 4
DK = 16
DV = 128
WIN = 64
F = 273


inv_root_two = 1.0 / math.sqrt(2.0)


def passed_along(block, axis, distance):
    devices = range(lax.axis_size(axis))
    route = [(i - distance, i) for i in devices if i - distance in devices]
    return lax.ppermute(block, axis, route)


def carried_in(part, axis, combine, identity):
    place = lax.axis_index(axis)
    gathered = jax.tree.map(lambda a: lax.all_gather(a, axis), part)
    state = jax.tree.map(lambda a, e: jnp.zeros_like(a) + jnp.asarray(e, a.dtype), part, identity)

    def one(step, state):
        return combine(
            state, jax.tree.map(lambda a: lax.dynamic_index_in_dim(a, step, 0, False), gathered)
        )

    return lax.fori_loop(0, place, one, state)


def features(inputs):
    row_count = inputs.shape[0]
    scaled = inputs.astype(jnp.float32).reshape(row_count, H, DK) * 0.5
    squares = (scaled[:, :, :, None] * scaled[:, :, None, :]).reshape(
        row_count, H, DK * DK
    ) * inv_root_two
    stacked = jnp.concatenate([jnp.ones((row_count, H, 1), jnp.float32), scaled, squares], axis=2)
    return jnp.transpose(stacked, (1, 2, 0)).astype(jnp.bfloat16)


def add_pairs(earlier, later):
    return (earlier[0] + later[0], earlier[1] + later[1])


def shards(query_rows, key_rows, value_rows):
    high = lax.Precision.HIGHEST
    length = query_rows.shape[0]
    block_rows = min(512, length)
    blocks = length // block_rows
    tail_rows = passed_along(
        (key_rows[length - WIN :], value_rows[length - WIN :]), ("outer", "inner"), 1
    )
    key_ext = jnp.concatenate([tail_rows[0], key_rows], axis=0)
    value_ext = jnp.concatenate([tail_rows[1], value_rows], axis=0)
    device = lax.axis_index(("outer", "inner"))
    key_feats = features(key_rows).reshape(H, F, blocks, block_rows)
    value_heads = value_rows.reshape(length, H, DV)
    value_ext_heads = value_ext.reshape(length + WIN, H, DV)
    per_block = jnp.einsum(
        "hfbt,bthv->bhfv",
        key_feats,
        value_heads.reshape(blocks, block_rows, H, DV),
        preferred_element_type=jnp.float32,
    )
    norm_blocks = jnp.transpose(jnp.sum(key_feats, axis=3, dtype=jnp.float32), (2, 0, 1))
    state_total = jnp.sum(per_block, axis=0)
    norm_total = jnp.sum(norm_blocks, axis=0)
    state_before = jnp.cumsum(per_block, axis=0) - per_block
    norm_before = jnp.cumsum(norm_blocks, axis=0) - norm_blocks
    empty_pair = (jnp.zeros_like(state_total), jnp.zeros_like(norm_total))
    column_part = carried_in((state_total, norm_total), "outer", add_pairs, empty_pair)
    inner_part = carried_in((state_total, norm_total), "inner", add_pairs, empty_pair)
    earlier_groups = lax.psum((column_part[0], column_part[1]), "inner")
    prefix = add_pairs(earlier_groups, inner_part)
    causal = jnp.arange(block_rows)[:, None] >= jnp.arange(block_rows)[None, :]
    offset = jnp.arange(block_rows + WIN)[None, :] - WIN - jnp.arange(block_rows)[:, None]
    query_heads = query_rows.reshape(block_rows, H, DK)
    key_heads = key_rows.reshape(block_rows, H, DK)
    query_feats = features(query_rows).astype(jnp.float32)
    state_now = prefix[0] + state_before[0]
    norm_now = prefix[1] + norm_before[0]
    numerator = jnp.einsum("hft,hfv->thv", query_feats, state_now, precision=high)
    denominator = jnp.einsum("hft,hf->th", query_feats, norm_now, precision=high)
    scores = (
        jnp.einsum("thd,shd->hts", query_heads, key_heads, preferred_element_type=jnp.float32)
        * 0.25
    )
    kernel = jnp.where(causal[None], 1.0 + scores + 0.5 * scores * scores, 0.0)
    numerator = numerator + jnp.einsum(
        "hts,shv->thv", kernel.astype(jnp.bfloat16), value_heads, preferred_element_type=jnp.float32
    )
    denominator = denominator + jnp.sum(kernel, axis=2).T
    linear_parts = (
        (numerator / denominator[:, :, None]).reshape(block_rows, H * DV).astype(jnp.bfloat16)
    )
    key_window = key_ext.reshape(block_rows + WIN, H, DK)
    wscores = (
        jnp.einsum("thd,shd->hts", query_heads, key_window, preferred_element_type=jnp.float32)
        * 0.25
    )
    global_key = device * length + 0 + jnp.arange(block_rows + WIN)[None, :] - WIN
    inside = (offset <= 0) & (offset >= -WIN) & (global_key >= 0)
    wscores = jnp.where(inside[None], wscores, -1e30)
    row_max = jnp.max(wscores, axis=2, keepdims=True)
    weights = jnp.exp(wscores - row_max)
    weights = weights / jnp.sum(weights, axis=2, keepdims=True)
    window_part = jnp.einsum(
        "hts,shv->thv",
        weights.astype(jnp.bfloat16),
        value_ext_heads,
        preferred_element_type=jnp.float32,
    )
    window_parts = window_part.reshape(block_rows, H * DV).astype(jnp.bfloat16)
    return (linear_parts, window_parts)


def solution(mesh):
    placed = (P(("outer", "inner"), None), P(("outer", "inner"), None), P(("outer", "inner"), None))
    return jax.shard_map(
        shards,
        mesh=mesh,
        in_specs=placed,
        out_specs=(P(("outer", "inner"), None), P(("outer", "inner"), None)),
        check_vma=False,
    )
```

profile of v0, /device:TPU:1, one launch (start us, length us, event | category | flops | bytes accessed | tf_op | source)
XLA Modules:
  0.0 167.9 jit_solution(8205172931582963198)
XLA Ops:
  7.2 0.0 all-gather.9.cloned.1.call-start
  7.2 0.8 bitcast_convert_fusion
  8.0 0.1 multiply_convert_fusion.1
  8.1 1.1 copy.25
  9.2 0.0 copy-start.3
  9.2 0.0 copy-start.2
  9.2 1.2 fusion.18
  10.5 0.0 copy-start.4
  10.5 0.0 all-gather.9.cloned.1.call-update
  10.5 0.0 all-gather.11.cloned.1.call-start
  10.6 0.7 all-gather.11.cloned.1.call-update
  11.3 0.0 all-reduce.2.cloned.1.call-start
  11.3 0.0 copy-done.3
  11.3 0.1 slice.7
  11.4 4.6 %collective-permute-start.1 = (bf16[64,64]{0,1:T(8,128)(2,1)S(1)}, bf16[64,64]{0,1:T(8,128)(2,1)S(1)}, u32[]{:S(2)}, u32[]{:S(2)}) collective-permute-start(bf16[64,64]{0,1:T(8,128)(2,1)S(1)} %slice.7), channel_id=1, source_target_pairs={{0,1},{1,2},{2,3},{3,4},{4,5},{5,6},{6,7},{7,8},{8,9},{9,10},{10,1... | collective-permute-start | bytes 24584 | tf_op jit(solution)/shard_map/ppermute | solution.py:21
  16.0 0.0 copy-done.2
  16.0 1.9 %collective-permute-start = (bf16[64,512]{1,0:T(8,128)(2,1)S(1)}, bf16[64,512]{1,0:T(8,128)(2,1)S(1)}, u32[]{:S(2)}, u32[]{:S(2)}) collective-permute-start(bf16[64,512]{1,0:T(8,128)(2,1)S(1)} %slice.6), channel_id=1, source_target_pairs={{0,1},{1,2},{2,3},{3,4},{4,5},{5,6},{6,7},{7,8},{8,9},{9,10},{10,1... | collective-permute-start | bytes 196616 | tf_op jit(solution)/shard_map/ppermute | solution.py:21
  18.0 0.4 convert_reduce_fusion
  18.4 0.2 fusion.17
  18.6 0.0 copy-done.4
  18.6 0.1 multiply_convert_fusion
  18.8 0.5 fusion.36
  19.3 0.2 convolution_bitcast_fusion
  19.5 14.6 %all-gather.5 = f32[8,4,273]{2,1,0:T(4,128)S(1)} all-gather(f32[1,4,273]{2,1,0:T(4,128)S(1)} %bitcast.104), channel_id=5, replica_groups=mesh['outer'=4,'inner'=8] {'inner'}, dimensions={0}, use_global_device_ids=true | all-gather | bytes 39312 | tf_op jit(solution)/shard_map/all_gather | solution.py:26
  34.1 7.3 %all-gather.4 = f32[4,4,273]{2,1,0:T(4,128)S(1)} all-gather(f32[1,4,273]{2,1,0:T(4,128)S(1)} %bitcast.105), channel_id=3, replica_groups=mesh['outer'=4,'inner'=8] {'outer'}, dimensions={0}, use_global_device_ids=true | all-gather | bytes 21840 | tf_op jit(solution)/shard_map/all_gather | solution.py:26
  41.4 0.0 collective-permute-done.1
  41.4 0.1 pad_maximum_fusion
  41.5 0.6 fusion.37
  42.2 0.0 collective-permute-done
  42.2 0.9 convolution_convert_fusion
  43.1 0.8 copy.21
  44.0 5.6 %all-gather.9.cloned.1.call-done = f32[16,273,128]{2,1,0:T(8,128)} async-done(((f32[4,273,128]{2,1,0:T(8,128)}), f32[16,273,128]{2,1,0:T(8,128)}) %all-gather.9.cloned.1.call-update) | async-done | bytes 2236432 | tf_op jit(solution)/shard_map/all_gather | solution.py:26
  49.7 0.0 copy-start
  49.7 14.1 %psum.15 = f32[4,273]{1,0:T(4,128)S(1)} all-reduce(f32[4,273]{1,0:T(4,128)S(1)} %get-tuple-element.72), channel_id=1, replica_groups=mesh['outer'=4,'inner'=8] {'inner'}, use_global_device_ids=true, to_apply=%region_6.7 | all-reduce | flops 1092 | bytes 8736 | tf_op jit(solution)/shard_map/psum | solution.py:79
  63.8 0.0 copy-done
  63.8 0.0 all-reduce.2.cloned.1.call-update
  63.8 38.3 %all-gather.11.cloned.1.call-done = f32[32,273,128]{2,1,0:T(8,128)} async-done(((f32[4,273,128]{2,1,0:T(8,128)}), f32[32,273,128]{2,1,0:T(8,128)}) %all-gather.11.cloned.1.call-update) | async-done | bytes 4472848 | tf_op jit(solution)/shard_map/all_gather | solution.py:26
  102.1 0.0 copy-start.1
  102.1 1.3 while.25
  102.2 1.2 bitcast_add_fusion.11
  103.4 0.5 fusion.19
  104.0 54.5 %all-reduce.2.cloned.1.call-done = f32[4,273,128]{2,1,0:T(8,128)} async-done(((f32[4,273,128]{2,1,0:T(8,128)}), f32[4,273,128]{2,1,0:T(8,128)}) %all-reduce.2.cloned.1.call-update) | async-done | bytes 559120 | tf_op jit(solution)/shard_map/psum | solution.py:79
  158.5 0.0 copy-done.1
  158.5 2.1 %fusion.7 = bf16[256,4,128]{0,2,1:T(8,128)(2,1)S(1)} fusion(f32[256,4,128]{0,2,1:T(8,128)S(1)} %convolution_bitcast_fusion, f32[4,273,128]{2,1,0:T(8,128)S(1)} %copy-done.1, f32[4,273,128]{2,1,0:T(8,128)} %all-reduce.2.cloned.1.call-done, f32[4,273,128]{2,1,0:T(8,128)S(1)} %get-tuple-element.71, bf16[256,4,256]{0,2,1:T(8,128)(2,1)S(1)} %bitcast.100, ...), kind=kOutput, calls=%fused_computation.15 | convolution fusion | flops 431881728 | bytes 3025442 | tf_op jit(solution)/shard_map/hft,hfv->thv/dot_general | solution.py:88
  160.6 0.8 copy.20
  (15 shorter events, 0.2 us)
Async XLA Ops:
  7.2 42.4 %all-gather.9.cloned.1.call-start = ((), (), s32[]{:S(2)}) async-start(), calls=%async_computation.1 | async-start | bytes 2867200 | tf_op jit(solution)/shard_map/all_gather | solution.py:26
  9.2 2.1 %copy-start.3 = (bf16[256,64]{0,1:T(8,128)(2,1)S(1)}, bf16[256,64]{0,1:T(8,128)(2,1)}, u32[]{:S(2)}) copy-start(bf16[256,64]{0,1:T(8,128)(2,1)} %param.8) | copy-start | bytes 98308
  9.2 6.8 %copy-start.2 = (bf16[256,512]{1,0:T(8,128)(2,1)S(1)}, bf16[256,512]{1,0:T(8,128)(2,1)}, u32[]{:S(2)}) copy-start(bf16[256,512]{1,0:T(8,128)(2,1)} %param.9) | copy-start | bytes 786436
  10.5 8.1 %copy-start.4 = (bf16[256,64]{0,1:T(8,128)(2,1)S(1)}, bf16[256,64]{0,1:T(8,128)(2,1)}, u32[]{:S(2)}) copy-start(bf16[256,64]{0,1:T(8,128)(2,1)} %param.7) | copy-start | bytes 98308
  10.5 91.5 %all-gather.11.cloned.1.call-start = ((), (), s32[]{:S(2)}) async-start(), calls=%async_computation.2 | async-start | bytes 5160960 | tf_op jit(solution)/shard_map/all_gather | solution.py:26
  11.3 147.2 %all-reduce.2.cloned.1.call-start = ((), (), s32[]{:S(2)}) async-start(), calls=%async_computation | async-start | bytes 1146880 | tf_op jit(solution)/shard_map/psum | solution.py:79
  11.4 30.0 %collective-permute-start.1 = (bf16[64,64]{0,1:T(8,128)(2,1)S(1)}, bf16[64,64]{0,1:T(8,128)(2,1)S(1)}, u32[]{:S(2)}, u32[]{:S(2)}) collective-permute-start(bf16[64,64]{0,1:T(8,128)(2,1)S(1)} %slice.7), channel_id=1, source_target_pairs={{0,1},{1,2},{2,3},{3,4},{4,5},{5,6},{6,7},{7,8},{8,9},{9,10},{10,1... | collective-permute-start | bytes 24584 | tf_op jit(solution)/shard_map/ppermute | solution.py:21
  16.0 26.2 %collective-permute-start = (bf16[64,512]{1,0:T(8,128)(2,1)S(1)}, bf16[64,512]{1,0:T(8,128)(2,1)S(1)}, u32[]{:S(2)}, u32[]{:S(2)}) collective-permute-start(bf16[64,512]{1,0:T(8,128)(2,1)S(1)} %slice.6), channel_id=1, source_target_pairs={{0,1},{1,2},{2,3},{3,4},{4,5},{5,6},{6,7},{7,8},{8,9},{9,10},{10,1... | collective-permute-start | bytes 196616 | tf_op jit(solution)/shard_map/ppermute | solution.py:21
  49.7 14.1 %copy-start = (f32[4,273,128]{2,1,0:T(8,128)}, f32[4,273,128]{2,1,0:T(8,128)S(1)}, u32[]{:S(2)}) copy-start(f32[4,273,128]{2,1,0:T(8,128)S(1)} %get-tuple-element.70) | copy-start | bytes 1677316
  102.1 56.4 %copy-start.1 = (f32[4,273,128]{2,1,0:T(8,128)S(1)}, f32[4,273,128]{2,1,0:T(8,128)}, u32[]{:S(2)}) copy-start(f32[4,273,128]{2,1,0:T(8,128)} %fusion.18) | copy-start | bytes 1677316
Sparse Core Ops, SparseCore 0:
  10.6 38.9 all-gather.8
  51.2 50.7 all-gather.10
  104.4 54.0 all-reduce.1
where the time goes:
time: 171 us; the launch traced here: 168 us
  waiting for transfers between devices  99.1 us (58%)
  blocking collectives  36 us (21%)
  between operations  14 us (8%)
  starting transfers between devices  6.61 us (4%)
  matrix products  6.15 us (4%)
  other arithmetic  3.03 us (2%)
  local copies, waits for them, and re-layouts  2.97 us (2%)
    psum x1, waiting for transfers between devices, shards(): earlier_groups = lax.psum((column_part[0], column_part[1]), 'inner')  54.5 us
    all_gather x2, waiting for transfers between devices, carried_in(): gathered = jax.tree.map(lambda a: lax.all_gather(a, axis), part)  43.9 us
    all_gather x2, blocking collectives, carried_in(): gathered = jax.tree.map(lambda a: lax.all_gather(a, axis), part)  21.9 us
    psum x1, blocking collectives, shards(): earlier_groups = lax.psum((column_part[0], column_part[1]), 'inner')  14.1 us
    ppermute x2, starting transfers between devices, passed_along(): return lax.ppermute(block, axis, route)  6.49 us
  transfers between devices with their start and end apart: 5, of which 3 were waited for; matrix products, arithmetic and copies ran while one was open for 4% of the time, Pallas kernels for 0%

commit v1 on v0

v1 whole, which is shorter than its diff:
```python
import functools
import math

import jax
import jax.numpy as jnp
from jax import lax
from jax.experimental import pallas as pl
from jax.experimental.pallas import tpu as pltpu
from jax.sharding import PartitionSpec as P

H = 4
DK = 16
DV = 128
WIN = 64
HALF_PAIRS = DK // 2
TAIL = DK + DK * HALF_PAIRS + HALF_PAIRS
ROWS = TAIL + 8
WIRE = jnp.float32

MESH = pl.DeviceIdType.MESH
inv_root_two = 1.0 / math.sqrt(2.0)


def feature_rows(scaled):
    parts = [scaled, scaled * scaled * inv_root_two]
    for d in range(1, HALF_PAIRS):
        rolled = jnp.concatenate([scaled[d:], scaled[:d]], axis=0)
        parts.append(scaled * rolled * inv_root_two)
    parts.append(scaled[:HALF_PAIRS] * scaled[HALF_PAIRS:] * inv_root_two)
    row = lax.broadcasted_iota(jnp.int32, (8, scaled.shape[1]), 0)
    parts.append(jnp.where(row == 0, 1.0, 0.0))
    return jnp.concatenate(parts, axis=0)


def dot(a, b, dims=((1,), (0,))):
    return lax.dot_general(a, b, (dims, ((), ())), preferred_element_type=jnp.float32)


def kernel(
    groups,
    inner,
    q_ref,
    k_ref,
    v_ref,
    lin_ref,
    win_ref,
    kext,
    vhalo,
    own,
    mate,
    tot,
    cols,
    gsum,
    gin,
    ret,
    pre,
    feats,
    num,
    den,
    halo_send,
    halo_recv,
    pair_send,
    pair_recv,
    col_send,
    col_recv,
    out_send,
    out_recv,
    ret_send,
    ret_recv,
    fwd_send,
    fwd_recv,
):
    f32, bf16 = jnp.float32, jnp.bfloat16
    length = q_ref.shape[0]
    n = inner // 2
    piece = tot.shape[1]
    half_rows = H // 2 * ROWS
    o = lax.axis_index("outer")
    i = lax.axis_index("inner")
    c = lax.rem(i, 2)
    z = lax.div(i, 2)
    flat = o * inner + i
    total = groups * inner
    nxt = lax.rem(flat + 1, total)
    prv = lax.rem(flat + total - 1, total)
    after = (lax.div(nxt, inner), lax.rem(nxt, inner))
    before = (lax.div(prv, inner), lax.rem(prv, inner))
    partner = (o, i + 1 - 2 * c)

    def chip(r):
        return lax.rem(z + r, n)

    column = [(o, chip(r) * 2 + c) for r in range(1, n)]
    others = [(lax.rem(o + r, groups), i) for r in range(1, groups)]

    barrier = pltpu.get_barrier_semaphore()
    peers = [partner, *column, *others, after, before]
    for peer in peers:
        pl.semaphore_signal(barrier, inc=1, device_id=peer, device_id_type=MESH)

    def remote(src, dst, send, recv, peer):
        return pltpu.make_async_remote_copy(
            src_ref=src, dst_ref=dst, send_sem=send, recv_sem=recv,
            device_id=peer, device_id_type=MESH,
        )

    keys = k_ref[...]
    keys_t = (keys.astype(f32) * 0.5).T
    ones = jnp.ones((8, length), bf16)
    row = lax.broadcasted_iota(jnp.int32, (8, DV), 0)
    rest = ROWS - DV

    def state(h):
        phi = feature_rows(keys_t[h * DK : (h + 1) * DK]).astype(bf16)
        part = dot(phi, v_ref[:, h * DV : (h + 1) * DV])
        norm = dot(ones, phi, ((1,), (1,)))
        high = jnp.concatenate([norm[:, DV:], jnp.zeros((8, DV - rest), f32)], axis=1)
        tail = jnp.where(row == 0, part[TAIL:], jnp.where(row == 1, norm[:, :DV], jnp.where(row == 2, high, 0.0)))
        first = h % 2 * ROWS
        own[h // 2, first : first + TAIL] = part[:TAIL]
        own[h // 2, first + TAIL : first + ROWS] = tail

    if own.shape[1] > half_rows:
        own[:, half_rows:] = jnp.zeros((2, own.shape[1] - half_rows, DV), f32)
    pair = [remote(own.at[j], mate.at[j], pair_send.at[j], pair_recv.at[j], partner) for j in range(2)]
    state(0)
    state(1)
    pl.semaphore_wait(barrier, len(peers))
    pair[0].start()
    state(2)
    state(3)
    pair[1].start()
    halo = [
        remote(k_ref.at[pl.ds(length - WIN, WIN)], kext, halo_send.at[0], halo_recv.at[0], after),
        remote(v_ref.at[pl.ds(length - WIN, WIN)], vhalo, halo_send.at[1], halo_recv.at[1], after),
    ]
    for copy in halo:
        copy.start()

    queries = q_ref[...]
    lane_head = lax.div(lax.broadcasted_iota(jnp.int32, queries.shape, 1), DK)

    def head_queries(h):
        return jnp.where(lane_head == h, queries, jnp.zeros_like(queries))

    def query_features():
        queries_t = (queries.astype(f32) * 0.5).T
        for h in range(H):
            phi = feature_rows(queries_t[h * DK : (h + 1) * DK])
            twice = lax.broadcasted_iota(jnp.int32, phi.shape, 0)
            weight = jnp.where((twice >= 2 * DK) & (twice < TAIL), 2.0, 1.0)
            feats[h] = (phi.astype(bf16).astype(f32) * weight).astype(bf16)

    step = 128

    def inside_block(h):
        q_h = head_queries(h)
        for first in range(0, length, step):
            end = first + step
            s = dot(q_h[first:end], keys[:end], ((1,), (1,))) * 0.25
            t_at = first + lax.broadcasted_iota(jnp.int32, s.shape, 0)
            u_at = lax.broadcasted_iota(jnp.int32, s.shape, 1)
            kern = jnp.where(t_at >= u_at, 1.0 + s + 0.5 * s * s, 0.0)
            den[h, first:end] = jnp.sum(kern, axis=1, keepdims=True)
            num[h, first:end] = dot(kern.astype(bf16), v_ref[:end, h * DV : (h + 1) * DV])

    def window(h):
        q_h = head_queries(h)
        at = slice(h * DV, (h + 1) * DV)
        for first in range(0, length, WIN):
            if first == 0:
                k_w = jnp.concatenate([kext[...], keys[:WIN]], axis=0)
                v_w = jnp.concatenate([vhalo[:, at], v_ref[:WIN, at]], axis=0)
            else:
                k_w = keys[first - WIN : first + WIN]
                v_w = v_ref[first - WIN : first + WIN, at]
            s = dot(q_h[first : first + WIN], k_w, ((1,), (1,))) * 0.25
            t_at = lax.broadcasted_iota(jnp.int32, s.shape, 0)
            u_at = lax.broadcasted_iota(jnp.int32, s.shape, 1)
            seen = (u_at >= t_at) & (u_at <= t_at + WIN)
            if first == 0:
                seen = seen & ((u_at >= WIN) | (flat > 0))
            s = jnp.where(seen, s, -1e30)
            e = jnp.exp(s - jnp.max(s, axis=1, keepdims=True))
            w = e / jnp.sum(e, axis=1, keepdims=True)
            win_ref[first : first + WIN, at] = dot(w.astype(bf16), v_w).astype(bf16)

    query_features()

    mine = remote(own.at[c], mate.at[c], pair_send.at[c], pair_recv.at[c], partner)
    mine.wait_recv()
    sums = own[c] + mate[c]
    tot[...] = sums.reshape(n, piece, DV).astype(tot.dtype)
    col = [
        remote(tot.at[chip(r)], cols.at[z], col_send.at[r - 1], col_recv.at[r - 1], column[r - 1])
        for r in range(1, n)
    ]
    for copy in col:
        copy.start()
    cols[z] = tot[z]
    inside_block(0)
    inside_block(1)
    inside_block(2)
    inside_block(3)
    for copy in col:
        copy.wait_recv()
    run = jnp.zeros((piece, DV), f32)
    befores = []
    for t in range(n):
        befores.append(run)
        run = run + cols[t].astype(f32)
    gsum[...] = run
    out = [
        remote(gsum, gin.at[r - 1], out_send.at[r - 1], out_recv.at[r - 1], others[r - 1])
        for r in range(1, groups)
    ]
    for copy in out:
        copy.start()
    for copy in halo:
        copy.wait()
    window(0)
    window(1)
    groups_before = jnp.zeros((piece, DV), f32)
    for r, copy in enumerate(out, 1):
        copy.wait_recv()
        groups_before = groups_before + jnp.where(r <= o, gin[r - 1], 0.0)
    for t in range(n):
        ret[t] = (befores[t] + groups_before).astype(ret.dtype)
    back = [
        remote(ret.at[chip(r)], pre.at[c, z], ret_send.at[r - 1], ret_recv.at[r - 1], column[r - 1])
        for r in range(1, n)
    ]
    for copy in back:
        copy.start()
    pre[c, z] = ret[z]

    def forward(r):
        src = lax.rem(z + n - r, n)
        return remote(pre.at[c, src], pre.at[c, src], fwd_send.at[r], fwd_recv.at[r], partner)

    fwd = [forward(r) for r in range(n)]
    fwd[0].start()
    window(2)
    window(3)
    for r in range(1, n):
        back[r - 1].wait_recv()
        fwd[r].start()
    other = remote(own.at[1 - c], mate.at[1 - c], pair_send.at[1 - c], pair_recv.at[1 - c], partner)
    other.wait_recv()
    for copy in fwd:
        copy.wait_recv()

    for h in range(H):
        first = h % 2 * ROWS
        held = pre[h // 2].reshape(n * piece, DV)[first : first + ROWS].astype(f32)
        held = held + jnp.where(c == 1, mate[h // 2, first : first + ROWS], 0.0)
        high = held.astype(bf16)
        low = (held - high.astype(f32)).astype(bf16)
        phi = feats[h]
        both = dot(phi, jnp.concatenate([high, low], axis=1), ((0,), (0,)))
        norm = jnp.concatenate([held[TAIL + 1 : TAIL + 2], held[TAIL + 2 : TAIL + 3, :rest]], axis=1)
        norm_high = norm.astype(bf16).astype(f32)
        norm_rows = jnp.concatenate([norm_high, norm - norm_high, jnp.zeros((6, ROWS), f32)], axis=0)
        bottom = dot(phi, norm_rows.astype(bf16), ((0,), (1,)))
        bottom = den[h] + bottom[:, 0:1] + bottom[:, 1:2]
        top = num[h] + both[:, :DV] + both[:, DV:]
        lin_ref[:, h * DV : (h + 1) * DV] = (top / bottom).astype(bf16)

    for copy in (*pair, *col, *out, *back, *fwd):
        copy.wait_send()


def shards(groups, inner, query_rows, key_rows, value_rows):
    length, width = value_rows.shape
    n = inner // 2
    half_rows = H // 2 * ROWS
    piece = -(-half_rows // (16 * n)) * 16
    f32 = jnp.float32
    dma = pltpu.SemaphoreType.DMA
    out = jax.ShapeDtypeStruct((length, width), jnp.bfloat16)
    vmem = pl.BlockSpec(memory_space=pltpu.VMEM)
    return pl.pallas_call(
        functools.partial(kernel, groups, inner),
        out_shape=(out, out),
        in_specs=[vmem] * 3,
        out_specs=(vmem, vmem),
        scratch_shapes=[
            pltpu.VMEM((WIN, H * DK), jnp.bfloat16),
            pltpu.VMEM((WIN, width), jnp.bfloat16),
            pltpu.VMEM((2, n * piece, DV), f32),
            pltpu.VMEM((2, n * piece, DV), f32),
            pltpu.VMEM((n, piece, DV), WIRE),
            pltpu.VMEM((n, piece, DV), WIRE),
            pltpu.VMEM((piece, DV), f32),
            pltpu.VMEM((groups - 1, piece, DV), f32),
            pltpu.VMEM((n, piece, DV), WIRE),
            pltpu.VMEM((2, n, piece, DV), WIRE),
            pltpu.VMEM((H, ROWS, length), jnp.bfloat16),
            pltpu.VMEM((H, length, DV), f32),
            pltpu.VMEM((H, length, 1), f32),
            dma((2,)), dma((2,)),
            dma((2,)), dma((2,)),
            dma((n - 1,)), dma((n - 1,)),
            dma((groups - 1,)), dma((groups - 1,)),
            dma((n - 1,)), dma((n - 1,)),
            dma((n,)), dma((n,)),
        ],
        compiler_params=pltpu.CompilerParams(collective_id=0, has_side_effects=True),
    )(query_rows, key_rows, value_rows)


def solution(mesh):
    rows = P(("outer", "inner"), None)
    return jax.shard_map(
        functools.partial(shards, mesh.shape["outer"], mesh.shape["inner"]),
        mesh=mesh,
        in_specs=(rows, rows, rows),
        out_specs=(rows, rows),
        check_vma=False,
    )
```

time: 171 us -> 29.2 us (0.17); the launches traced: 168 us -> 28.9 us
  waiting for transfers between devices: 99.1 us -> 0 us
  blocking collectives: 36 us -> 0 us
  Pallas kernels: 0 us -> 23.6 us
  between operations: 14 us -> 0.66 us
  starting transfers between devices: 6.61 us -> 0 us
  matrix products: 6.15 us -> 0 us
  other arithmetic: 3.03 us -> 0 us
    psum x1 -> x0, waiting for transfers between devices: 54.5 us -> none  [shards(): earlier_groups = lax.psum((column_part[0], column_part[1]), 'inner')]
    all_gather x2 -> x0, waiting for transfers between devices: 43.9 us -> none  [carried_in(): gathered = jax.tree.map(lambda a: lax.all_gather(a, axis), part)]
    pallas_call x0 -> x1, Pallas kernels: none -> 23.6 us  [shards(): pl.pallas_call(functools.partial(kernel, groups, inner), out_shape=(out,...]
    all_gather x2 -> x0, blocking collectives: 21.9 us -> none  [carried_in(): gathered = jax.tree.map(lambda a: lax.all_gather(a, axis), part)]
    psum x1 -> x0, blocking collectives: 14.1 us -> none  [shards(): earlier_groups = lax.psum((column_part[0], column_part[1]), 'inner')]
    ppermute x2 -> x0, starting transfers between devices: 6.49 us -> none  [passed_along(): return lax.ppermute(block, axis, route)]
    dot_general x6 -> x0, matrix products: 5.51 us -> none  [the longest x1 2.07 us: shards(): jnp.einsum('hft,hfv->thv', query_feats, state_now, precision=high)]
    unnamed x12 -> x8, local copies, waits for them, and re-layouts: 1.71 us -> 4.65 us
  transfers between devices with their start and end apart: 5 -> 0, of which waited for: 3 -> 0; matrix products, arithmetic and copies ran while one was open for 4% -> 0% of each run, Pallas kernels for 0% -> 0%
where the time goes in v1:
time: 29.2 us; the launch traced here: 28.9 us
  Pallas kernels  23.6 us (81%)
  local copies, waits for them, and re-layouts  4.65 us (16%)
  between operations  0.66 us (2%)
    pallas_call x1, Pallas kernels, shards(): pl.pallas_call(functools.partial(kernel, groups, inner), out_shape=(out,...  23.6 us
    unnamed x8, local copies, waits for them, and re-layouts  4.65 us

profile of v1, /device:TPU:1, one launch (start us, length us, event | category | flops | bytes accessed | tf_op | source)
XLA Modules:
  0.0 28.9 jit_solution(14570717114988257596)
XLA Ops:
  0.6 0.0 copy-start.1
  0.6 1.5 %copy.5.q_ref = bf16[256,64]{1,0:T(8,128)(2,1)} copy(bf16[256,64]{0,1:T(8,128)(2,1)} %param.3) | data formatting | bytes 65536 | tf_op args[0]
  2.1 0.0 copy-done.1
  2.1 0.7 %copy.6.k_ref = bf16[256,64]{1,0:T(8,128)(2,1)} copy(bf16[256,64]{0,1:T(8,128)(2,1)S(1)} %copy-done.1) | data formatting | bytes 65536 | tf_op args[1]
  2.9 23.6 %shard_map.50 = (bf16[256,512]{1,0:T(8,128)(2,1)}, bf16[256,512]{1,0:T(8,128)(2,1)}) custom-call(bf16[256,64]{1,0:T(8,128)(2,1)} %copy.5.q_ref, bf16[256,64]{1,0:T(8,128)(2,1)} %copy.6.k_ref, bf16[256,512]{1,0:T(8,128)(2,1)} %v_ref.1), custom_call_target="tpu_custom_call" | custom-call | tf_op jit(solution)/shard_map/pallas_call | solution.py:282
  26.5 0.0 copy-start
  26.5 1.7 %copy.9 = bf16[256,512]{1,0:T(8,128)(2,1)} copy(bf16[256,512]{1,0:T(8,128)(2,1)} %get-tuple-element.4) | data formatting | bytes 524288
  28.2 0.0 copy-done
  28.2 0.7 %copy.10 = bf16[256,512]{1,0:T(8,128)(2,1)} copy(bf16[256,512]{1,0:T(8,128)(2,1)S(1)} %copy-done) | data formatting | bytes 524288
Async XLA Ops:
  0.6 1.5 %copy-start.1 = (bf16[256,64]{0,1:T(8,128)(2,1)S(1)}, bf16[256,64]{0,1:T(8,128)(2,1)}, u32[]{:S(2)}) copy-start(bf16[256,64]{0,1:T(8,128)(2,1)} %param.4) | copy-start | bytes 98308
  26.5 1.7 %copy-start = (bf16[256,512]{1,0:T(8,128)(2,1)S(1)}, bf16[256,512]{1,0:T(8,128)(2,1)}, u32[]{:S(2)}) copy-start(bf16[256,512]{1,0:T(8,128)(2,1)} %get-tuple-element.5) | copy-start | bytes 786436

commit v2 on v1

--- a/solution.py
+++ b/solution.py
@@ -71,7 +71,7 @@
     fwd_recv,
 ):
     f32, bf16 = jnp.float32, jnp.bfloat16
-    length = q_ref.shape[0]
+    length = q_ref.shape[1]
     n = inner // 2
     piece = tot.shape[1]
     half_rows = H // 2 * ROWS
@@ -104,11 +104,11 @@
             device_id=peer, device_id_type=MESH,
         )
 
-    keys = k_ref[...]
-    keys_t = (keys.astype(f32) * 0.5).T
+    keys_t = k_ref[...].astype(f32) * 0.5
     ones = jnp.ones((8, length), bf16)
     row = lax.broadcasted_iota(jnp.int32, (8, DV), 0)
     rest = ROWS - DV
+    step = 2 * WIN
 
     def state(h):
         phi = feature_rows(keys_t[h * DK : (h + 1) * DK]).astype(bf16)
@@ -131,27 +131,26 @@
     state(3)
     pair[1].start()
     halo = [
-        remote(k_ref.at[pl.ds(length - WIN, WIN)], kext, halo_send.at[0], halo_recv.at[0], after),
+        remote(k_ref.at[:, pl.ds(length - step, step)], kext, halo_send.at[0], halo_recv.at[0], after),
         remote(v_ref.at[pl.ds(length - WIN, WIN)], vhalo, halo_send.at[1], halo_recv.at[1], after),
     ]
     for copy in halo:
         copy.start()
 
-    queries = q_ref[...]
+    queries = q_ref[...].astype(f32).T.astype(bf16)
+    keys = k_ref[...].astype(f32).T.astype(bf16)
     lane_head = lax.div(lax.broadcasted_iota(jnp.int32, queries.shape, 1), DK)
 
     def head_queries(h):
         return jnp.where(lane_head == h, queries, jnp.zeros_like(queries))
 
     def query_features():
-        queries_t = (queries.astype(f32) * 0.5).T
+        queries_t = q_ref[...].astype(f32) * 0.5
         for h in range(H):
             phi = feature_rows(queries_t[h * DK : (h + 1) * DK])
             twice = lax.broadcasted_iota(jnp.int32, phi.shape, 0)
             weight = jnp.where((twice >= 2 * DK) & (twice < TAIL), 2.0, 1.0)
             feats[h] = (phi.astype(bf16).astype(f32) * weight).astype(bf16)
-
-    step = 128
 
     def inside_block(h):
         q_h = head_queries(h)
@@ -169,7 +168,7 @@
         at = slice(h * DV, (h + 1) * DV)
         for first in range(0, length, WIN):
             if first == 0:
-                k_w = jnp.concatenate([kext[...], keys[:WIN]], axis=0)
+                k_w = jnp.concatenate([kext[...].astype(f32).T[step - WIN :].astype(bf16), keys[:WIN]], axis=0)
                 v_w = jnp.concatenate([vhalo[:, at], v_ref[:WIN, at]], axis=0)
             else:
                 k_w = keys[first - WIN : first + WIN]
@@ -277,7 +276,7 @@
     piece = -(-half_rows // (16 * n)) * 16
     f32 = jnp.float32
     dma = pltpu.SemaphoreType.DMA
-    out = jax.ShapeDtypeStruct((length, width), jnp.bfloat16)
+    out = pltpu.VMEM((length, width), jnp.bfloat16)
     vmem = pl.BlockSpec(memory_space=pltpu.VMEM)
     return pl.pallas_call(
         functools.partial(kernel, groups, inner),
@@ -285,7 +284,7 @@
         in_specs=[vmem] * 3,
         out_specs=(vmem, vmem),
         scratch_shapes=[
-            pltpu.VMEM((WIN, H * DK), jnp.bfloat16),
+            pltpu.VMEM((H * DK, 2 * WIN), jnp.bfloat16),
             pltpu.VMEM((WIN, width), jnp.bfloat16),
             pltpu.VMEM((2, n * piece, DV), f32),
             pltpu.VMEM((2, n * piece, DV), f32),
@@ -306,7 +305,7 @@
             dma((n,)), dma((n,)),
         ],
         compiler_params=pltpu.CompilerParams(collective_id=0, has_side_effects=True),
-    )(query_rows, key_rows, value_rows)
+    )(query_rows.T, key_rows.T, value_rows)
 
 
 def solution(mesh):

time: 29.2 us -> 25 us (0.86)
  local copies, waits for them, and re-layouts: 4.65 us -> 1.41 us
  Pallas kernels: 23.6 us -> 22.8 us
    unnamed x8 -> x2, local copies, waits for them, and re-layouts: 4.65 us -> 1.41 us
    pallas_call x1, Pallas kernels: 23.6 us -> 22.8 us  [shards(): pl.pallas_call(functools.partial(kernel, groups, inner), out_shape=(out,...]
where the time goes in v2:
time: 25 us; the launch traced here: 24.9 us
  Pallas kernels  22.8 us (91%)
  local copies, waits for them, and re-layouts  1.41 us (6%)
  between operations  0.64 us (3%)
    pallas_call x1, Pallas kernels, shards(): pl.pallas_call(functools.partial(kernel, groups, inner), out_shape=(out,...  22.8 us
    unnamed x2, local copies, waits for them, and re-layouts  1.41 us

profile of v2, /device:TPU:1, one launch (start us, length us, event | category | flops | bytes accessed | tf_op | source)
XLA Modules:
  0.0 24.9 jit_solution(14763814200311646874)
XLA Ops:
  0.6 22.8 %shard_map.50 = (bf16[256,512]{1,0:T(8,128)(2,1)S(1)}, bf16[256,512]{1,0:T(8,128)(2,1)S(1)}) custom-call(bf16[64,256]{1,0:T(8,128)(2,1)} %bitcast.2, bf16[64,256]{1,0:T(8,128)(2,1)} %bitcast.3, bf16[256,512]{1,0:T(8,128)(2,1)} %v_ref.1), custom_call_target="tpu_custom_call" | custom-call | tf_op jit(solution)/shard_map/pallas_call | solution.py:281
  23.5 0.7 %copy.7 = bf16[256,512]{1,0:T(8,128)(2,1)} copy(bf16[256,512]{1,0:T(8,128)(2,1)S(1)} %get-tuple-element.2) | data formatting | bytes 524288
  24.2 0.7 %copy.8 = bf16[256,512]{1,0:T(8,128)(2,1)} copy(bf16[256,512]{1,0:T(8,128)(2,1)S(1)} %get-tuple-element.3) | data formatting | bytes 524288

commit v3 on v2

--- a/solution.py
+++ b/solution.py
@@ -16,6 +16,7 @@
 TAIL = DK + DK * HALF_PAIRS + HALF_PAIRS
 ROWS = TAIL + 8
 WIRE = jnp.float32
+SPLIT = 4
 
 MESH = pl.DeviceIdType.MESH
 inv_root_two = 1.0 / math.sqrt(2.0)
@@ -52,6 +53,8 @@
     cols,
     gsum,
     gin,
+    gsum_before,
+    befores,
     ret,
     pre,
     feats,
@@ -69,6 +72,8 @@
     ret_recv,
     fwd_send,
     fwd_recv,
+    hello,
+    go,
 ):
     f32, bf16 = jnp.float32, jnp.bfloat16
     length = q_ref.shape[1]
@@ -82,21 +87,34 @@
     flat = o * inner + i
     total = groups * inner
     nxt = lax.rem(flat + 1, total)
-    prv = lax.rem(flat + total - 1, total)
     after = (lax.div(nxt, inner), lax.rem(nxt, inner))
-    before = (lax.div(prv, inner), lax.rem(prv, inner))
     partner = (o, i + 1 - 2 * c)
 
     def chip(r):
         return lax.rem(z + r, n)
 
-    column = [(o, chip(r) * 2 + c) for r in range(1, n)]
-    others = [(lax.rem(o + r, groups), i) for r in range(1, groups)]
-
     barrier = pltpu.get_barrier_semaphore()
-    peers = [partner, *column, *others, after, before]
-    for peer in peers:
-        pl.semaphore_signal(barrier, inc=1, device_id=peer, device_id_type=MESH)
+    mates = [(o, chip(r) * 2 + 1) for r in range(1, n)]
+    crowd = [(lax.rem(o + r, groups), z * 2 + 1) for r in range(1, groups)]
+    chips = total // 2
+    here = o * n + z
+    ends = [lax.rem(here + 1, chips), lax.rem(here + chips - 1, chips)]
+    peers = [*mates, *crowd, *[(lax.div(e, n), lax.rem(e, n) * 2 + 1) for e in ends]]
+
+    @pl.when(c == 1)
+    def _():
+        pl.semaphore_signal(barrier, inc=1, device_id=partner, device_id_type=MESH)
+
+    @pl.when(c == 0)
+    def _():
+        pl.semaphore_wait(barrier, 1)
+        pl.semaphore_signal(hello, inc=1, device_id=partner, device_id_type=MESH)
+
+    @pl.when(c == 1)
+    def _():
+        pl.semaphore_wait(hello, 1)
+        for peer in peers:
+            pl.semaphore_signal(barrier, inc=1, device_id=peer, device_id_type=MESH)
 
     def remote(src, dst, send, recv, peer):
         return pltpu.make_async_remote_copy(
@@ -104,38 +122,42 @@
             device_id=peer, device_id_type=MESH,
         )
 
-    keys_t = k_ref[...].astype(f32) * 0.5
     ones = jnp.ones((8, length), bf16)
     row = lax.broadcasted_iota(jnp.int32, (8, DV), 0)
     rest = ROWS - DV
     step = 2 * WIN
 
-    def state(h):
-        phi = feature_rows(keys_t[h * DK : (h + 1) * DK]).astype(bf16)
-        part = dot(phi, v_ref[:, h * DV : (h + 1) * DV])
+    def state(half, j):
+        h = half * (H // 2) + j
+        scaled = k_ref[pl.ds(pl.multiple_of(h * DK, DK), DK), :].astype(f32) * 0.5
+        phi = feature_rows(scaled).astype(bf16)
+        part = dot(phi, v_ref[:, pl.ds(pl.multiple_of(h * DV, DV), DV)])
         norm = dot(ones, phi, ((1,), (1,)))
         high = jnp.concatenate([norm[:, DV:], jnp.zeros((8, DV - rest), f32)], axis=1)
         tail = jnp.where(row == 0, part[TAIL:], jnp.where(row == 1, norm[:, :DV], jnp.where(row == 2, high, 0.0)))
-        first = h % 2 * ROWS
-        own[h // 2, first : first + TAIL] = part[:TAIL]
-        own[h // 2, first + TAIL : first + ROWS] = tail
+        first = j * ROWS
+        own[half, first : first + TAIL] = part[:TAIL]
+        own[half, first + TAIL : first + ROWS] = tail
 
     if own.shape[1] > half_rows:
         own[:, half_rows:] = jnp.zeros((2, own.shape[1] - half_rows, DV), f32)
-    pair = [remote(own.at[j], mate.at[j], pair_send.at[j], pair_recv.at[j], partner) for j in range(2)]
-    state(0)
-    state(1)
-    pl.semaphore_wait(barrier, len(peers))
-    pair[0].start()
-    state(2)
-    state(3)
-    pair[1].start()
+        mate[:, half_rows:] = jnp.zeros((2, own.shape[1] - half_rows, DV), f32)
+    pair = []
+    for j in range(H // 2):
+        state(1 - c, j)
+        at = pl.ds(j * ROWS, ROWS)
+        pair.append(
+            remote(own.at[1 - c, at], mate.at[1 - c, at], pair_send.at[j], pair_recv.at[j], partner)
+        )
+        pair[j].start()
+    for j in range(H // 2):
+        state(c, j)
+    at = pl.ds(0, half_rows)
+    spare = remote(own.at[0, at], mate.at[0, at], pair_send.at[H // 2], pair_recv.at[H // 2], partner)
     halo = [
         remote(k_ref.at[:, pl.ds(length - step, step)], kext, halo_send.at[0], halo_recv.at[0], after),
         remote(v_ref.at[pl.ds(length - WIN, WIN)], vhalo, halo_send.at[1], halo_recv.at[1], after),
     ]
-    for copy in halo:
-        copy.start()
 
     queries = q_ref[...].astype(f32).T.astype(bf16)
     keys = k_ref[...].astype(f32).T.astype(bf16)
@@ -186,68 +208,118 @@
 
     query_features()
 
-    mine = remote(own.at[c], mate.at[c], pair_send.at[c], pair_recv.at[c], partner)
-    mine.wait_recv()
-    sums = own[c] + mate[c]
-    tot[...] = sums.reshape(n, piece, DV).astype(tot.dtype)
-    col = [
-        remote(tot.at[chip(r)], cols.at[z], col_send.at[r - 1], col_recv.at[r - 1], column[r - 1])
-        for r in range(1, n)
-    ]
-    for copy in col:
+    @pl.when(c == 1)
+    def _():
+        pl.semaphore_wait(barrier, len(peers))
+        pl.semaphore_signal(go, inc=1, device_id=partner, device_id_type=MESH)
+
+    @pl.when(c == 0)
+    def _():
+        pl.semaphore_wait(go, 1)
+
+    def column_copy(t):
+        return remote(tot.at[t], cols.at[z], col_send.at[t], col_recv.at[z], (o, t * 2 + c))
+
+    def column_arrival(t):
+        return remote(tot.at[t], cols.at[t], col_send.at[t], col_recv.at[t], (o, t * 2 + c))
+
+    def far_first(k):
+        return jnp.where(z < n // 2, n - 1 - k, k)
+
+    for j in range(H // 2):
+        pair[j].wait_recv()
+    tot[...] = (own[c] + mate[c]).reshape(n, piece, DV).astype(tot.dtype)
+    for k in range(n):
+        t = far_first(k)
+
+        @pl.when(z != t)
+        def _(t=t):
+            column_copy(t).start()
+
+    @pl.when(c == 0)
+    def _():
+        spare.start()
+
+    for copy in halo:
         copy.start()
     cols[z] = tot[z]
     inside_block(0)
     inside_block(1)
     inside_block(2)
     inside_block(3)
-    for copy in col:
-        copy.wait_recv()
+    for t in range(n):
+        @pl.when(z != t)
+        def _(t=t):
+            column_arrival(t).wait_recv()
+
     run = jnp.zeros((piece, DV), f32)
-    befores = []
     for t in range(n):
-        befores.append(run)
+        befores[t] = run
         run = run + cols[t].astype(f32)
     gsum[...] = run
-    out = [
-        remote(gsum, gin.at[r - 1], out_send.at[r - 1], out_recv.at[r - 1], others[r - 1])
-        for r in range(1, groups)
-    ]
-    for copy in out:
-        copy.start()
+    def group_copy(g, k):
+        return remote(gsum, gin.at[o], out_send.at[k], out_recv.at[o], (g, i))
+
+    later = []
+    for r in range(1, groups):
+        g = lax.rem(o + jnp.where(lax.rem(o, 2) == 0, groups - r, r), groups)
+        later.append(g)
+
+        @pl.when(g > o)
+        def _(g=g, r=r):
+            group_copy(g, r - 1).start()
+
     for copy in halo:
         copy.wait()
     window(0)
+    gsum_before[...] = jnp.zeros((piece, DV), f32)
+    for g in range(groups - 1):
+        @pl.when(g < o)
+        def _(g=g):
+            remote(gsum, gin.at[g], out_send.at[0], out_recv.at[g], (g, i)).wait_recv()
+            gsum_before[...] += gin[g]
+
+    groups_before = gsum_before[...]
+
+    def back_copy(t):
+        return remote(ret.at[t], pre.at[c, z], ret_send.at[t], ret_recv.at[z], (o, t * 2 + c))
+
+    def back_arrival(t):
+        return remote(ret.at[t], pre.at[c, t], ret_send.at[t], ret_recv.at[t], (o, t * 2 + c))
+
+    for k in range(n):
+        t = far_first(k)
+        ret[t] = (befores[t] + groups_before).astype(ret.dtype)
+
+        @pl.when(z != t)
+        def _(t=t):
+            back_copy(t).start()
+
+    pre[c, z] = ret[z]
+
+    def forward(t):
+        return remote(pre.at[c, t], pre.at[c, t], fwd_send.at[t], fwd_recv.at[t], partner)
+
+    def forward_arrival(t):
+        return remote(pre.at[1 - c, t], pre.at[1 - c, t], fwd_send.at[t], fwd_recv.at[t], partner)
+
+    forward(z).start()
     window(1)
-    groups_before = jnp.zeros((piece, DV), f32)
-    for r, copy in enumerate(out, 1):
-        copy.wait_recv()
-        groups_before = groups_before + jnp.where(r <= o, gin[r - 1], 0.0)
-    for t in range(n):
-        ret[t] = (befores[t] + groups_before).astype(ret.dtype)
-    back = [
-        remote(ret.at[chip(r)], pre.at[c, z], ret_send.at[r - 1], ret_recv.at[r - 1], column[r - 1])
-        for r in range(1, n)
-    ]
-    for copy in back:
-        copy.start()
-    pre[c, z] = ret[z]
-
-    def forward(r):
-        src = lax.rem(z + n - r, n)
-        return remote(pre.at[c, src], pre.at[c, src], fwd_send.at[r], fwd_recv.at[r], partner)
-
-    fwd = [forward(r) for r in range(n)]
-    fwd[0].start()
     window(2)
     window(3)
-    for r in range(1, n):
-        back[r - 1].wait_recv()
-        fwd[r].start()
-    other = remote(own.at[1 - c], mate.at[1 - c], pair_send.at[1 - c], pair_recv.at[1 - c], partner)
-    other.wait_recv()
-    for copy in fwd:
-        copy.wait_recv()
+    for d in range(1, n):
+        for t in (z - d, z + d):
+            @pl.when((t >= 0) & (t < n))
+            def _(t=t):
+                back_arrival(t).wait_recv()
+                forward(t).start()
+
+    @pl.when(c == 1)
+    def _():
+        spare.wait_recv()
+
+    for t in range(n):
+        forward_arrival(t).wait_recv()
 
     for h in range(H):
         first = h % 2 * ROWS
@@ -265,8 +337,36 @@
         top = num[h] + both[:, :DV] + both[:, DV:]
         lin_ref[:, h * DV : (h + 1) * DV] = (top / bottom).astype(bf16)
 
-    for copy in (*pair, *col, *out, *back, *fwd):
+    @pl.when(c == 0)
+    def _():
+        spare.wait_send()
+
+    for t in range(n):
+        @pl.when(z != t)
+        def _(t=t):
+            column_copy(t).wait_send()
+            back_copy(t).wait_send()
+
+        forward(t).wait_send()
+    for k, g in enumerate(later):
+        @pl.when(g > o)
+        def _(g=g, k=k):
+            group_copy(g, k).wait_send()
+
+    for copy in pair:
         copy.wait_send()
+
+
+def place(lin_vmem, win_vmem, lin_out, win_out, sems):
+    rows = lin_vmem.shape[0] // SPLIT
+    copies = []
+    for a, (src, dst) in enumerate(((lin_vmem, lin_out), (win_vmem, win_out))):
+        for b in range(SPLIT):
+            at = pl.ds(b * rows, rows)
+            copies.append(pltpu.make_async_copy(src.at[at], dst.at[at], sems.at[a, b]))
+            copies[-1].start()
+    for copy in copies:
+        copy.wait()
 
 
 def shards(groups, inner, query_rows, key_rows, value_rows):
@@ -278,7 +378,7 @@
     dma = pltpu.SemaphoreType.DMA
     out = pltpu.VMEM((length, width), jnp.bfloat16)
     vmem = pl.BlockSpec(memory_space=pltpu.VMEM)
-    return pl.pallas_call(
+    held = pl.pallas_call(
         functools.partial(kernel, groups, inner),
         out_shape=(out, out),
         in_specs=[vmem] * 3,
@@ -291,21 +391,33 @@
             pltpu.VMEM((n, piece, DV), WIRE),
             pltpu.VMEM((n, piece, DV), WIRE),
             pltpu.VMEM((piece, DV), f32),
-            pltpu.VMEM((groups - 1, piece, DV), f32),
+            pltpu.VMEM((groups, piece, DV), f32),
+            pltpu.VMEM((piece, DV), f32),
+            pltpu.VMEM((n, piece, DV), f32),
             pltpu.VMEM((n, piece, DV), WIRE),
             pltpu.VMEM((2, n, piece, DV), WIRE),
             pltpu.VMEM((H, ROWS, length), jnp.bfloat16),
             pltpu.VMEM((H, length, DV), f32),
             pltpu.VMEM((H, length, 1), f32),
             dma((2,)), dma((2,)),
-            dma((2,)), dma((2,)),
-            dma((n - 1,)), dma((n - 1,)),
-            dma((groups - 1,)), dma((groups - 1,)),
-            dma((n - 1,)), dma((n - 1,)),
+            dma((H // 2 + 1,)), dma((H // 2 + 1,)),
             dma((n,)), dma((n,)),
+            dma((groups - 1,)), dma((groups,)),
+            dma((n,)), dma((n,)),
+            dma((n,)), dma((n,)),
+            pltpu.SemaphoreType.REGULAR, pltpu.SemaphoreType.REGULAR,
         ],
         compiler_params=pltpu.CompilerParams(collective_id=0, has_side_effects=True),
     )(query_rows.T, key_rows.T, value_rows)
+    hbm = pl.BlockSpec(memory_space=pl.ANY)
+    placed = jax.ShapeDtypeStruct((length, width), jnp.bfloat16)
+    return pl.pallas_call(
+        place,
+        out_shape=(placed, placed),
+        in_specs=[vmem] * 2,
+        out_specs=(hbm, hbm),
+        scratch_shapes=[dma((2, SPLIT))],
+    )(*[pltpu.with_memory_space_constraint(x, pltpu.VMEM) for x in held])
 
 
 def solution(mesh):

time: 25 us -> 23 us (0.920)
  local copies, waits for them, and re-layouts: 1.41 us -> 0 us
  Pallas kernels: 22.8 us -> 22.2 us
    pallas_call x1, Pallas kernels: 22.8 us -> 21.3 us  [shards(): pl.pallas_call(functools.partial(kernel, groups, inner), out_shape=(out,...]
    unnamed x2 -> x0, local copies, waits for them, and re-layouts: 1.41 us -> none
    pallas_call x0 -> x1, Pallas kernels: none -> 0.85 us  [shards(): pl.pallas_call(place, out_shape=(placed, placed), in_specs=[vmem] * 2, ou...]
where the time goes in v3:
time: 23 us; the launch traced here: 22.8 us
  Pallas kernels  22.2 us (97%)
  between operations  0.64 us (3%)
    pallas_call x1, Pallas kernels, shards(): pl.pallas_call(functools.partial(kernel, groups, inner), out_shape=(out,...  21.3 us
    pallas_call x1, Pallas kernels, shards(): pl.pallas_call(place, out_shape=(placed, placed), in_specs=[vmem] * 2, ou...  0.85 us

profile of v3, /device:TPU:1, one launch (start us, length us, event | category | flops | bytes accessed | tf_op | source)
XLA Modules:
  0.0 22.8 jit_solution(2854444742827504676)
XLA Ops:
  0.6 21.3 %shard_map.50 = (bf16[256,512]{1,0:T(8,128)(2,1)S(1)}, bf16[256,512]{1,0:T(8,128)(2,1)S(1)}) custom-call(bf16[64,256]{1,0:T(8,128)(2,1)} %bitcast.2, bf16[64,256]{1,0:T(8,128)(2,1)} %bitcast.3, bf16[256,512]{1,0:T(8,128)(2,1)} %v_ref.1), custom_call_target="tpu_custom_call" | custom-call | tf_op jit(solution)/shard_map/pallas_call | solution.py:381
  22.0 0.9 %shard_map.51 = (bf16[256,512]{1,0:T(8,128)(2,1)}, bf16[256,512]{1,0:T(8,128)(2,1)}) custom-call(bf16[256,512]{1,0:T(8,128)(2,1)S(1)} %get-tuple-element.4.lin_vmem, bf16[256,512]{1,0:T(8,128)(2,1)S(1)} %get-tuple-element.5.win_vmem), custom_call_target="tpu_custom_call" | custom-call | tf_op jit(solution)/shard_map/pallas_call | solution.py:414
